TPU v7x, 32 devices: a whole 2x2x4 slice. The times are simulated.
32 devices in a mesh: dp: 8 (over y, x, core), tensor: 4 (over z).
Axes of the slice: x: 2, y: 2, z: 4, core: 2. Of those that a mesh axis runs over, the one named last changes fastest.
Arguments:
- grad_inproj: bfloat16 [8, 768, 2304], P('dp', None, 'tensor'), may hold values from -32 to 32
- error_inproj: float32 [8, 768, 2304], P('dp', None, 'tensor'), may hold values from -3 to 3
- basis_inproj: float32 [2304, 32], P('tensor'), may hold values from -6 to 6
- weight_inproj: float32 [768, 2304], P('dp', 'tensor'), may hold values from -0.3 to 0.3
- moment_inproj: float32 [768, 2304], P('dp', 'tensor'), may hold values from -0.3 to 0.3
- grad_outproj: bfloat16 [8, 768, 768], P('dp', 'tensor'), may hold values from -32 to 32
- error_outproj: float32 [8, 768, 768], P('dp', 'tensor'), may hold values from -3 to 3
- basis_outproj: float32 [768, 32], replicated, may hold values from -6 to 6
- weight_outproj: float32 [768, 768], P(('tensor', 'dp')), may hold values from -0.3 to 0.3
- moment_outproj: float32 [768, 768], P(('tensor', 'dp')), may hold values from -0.3 to 0.3
- grad_expand: bfloat16 [8, 768, 3072], P('dp', None, 'tensor'), may hold values from -32 to 32
- error_expand: float32 [8, 768, 3072], P('dp', None, 'tensor'), may hold values from -3 to 3
- basis_expand: float32 [3072, 32], P('tensor'), may hold values from -6 to 6
- weight_expand: float32 [768, 3072], P('dp', 'tensor'), may hold values from -0.3 to 0.3
- moment_expand: float32 [768, 3072], P('dp', 'tensor'), may hold values from -0.3 to 0.3
- grad_contract: bfloat16 [8, 3072, 768], P('dp', 'tensor'), may hold values from -32 to 32
- error_contract: float32 [8, 3072, 768], P('dp', 'tensor'), may hold values from -3 to 3
- basis_contract: float32 [768, 32], replicated, may hold values from -6 to 6
- weight_contract: float32 [3072, 768], P(('tensor', 'dp')), may hold values from -0.3 to 0.3
- moment_contract: float32 [3072, 768], P(('tensor', 'dp')), may hold values from -0.3 to 0.3
Outputs:
- residue_inproj: float32 [8, 768, 2304], P('dp', None, 'tensor')
- factor_inproj: float32 [2304, 32], P('tensor')
- master_inproj: float32 [768, 2304], P('dp', 'tensor')
- velocity_inproj: float32 [768, 2304], P('dp', 'tensor')
- serving_inproj: bfloat16 [768, 2304], P(None, 'tensor')
- residue_outproj: float32 [8, 768, 768], P('dp', 'tensor')
- factor_outproj: float32 [768, 32], replicated
- master_outproj: float32 [768, 768], P(('tensor', 'dp'))
- velocity_outproj: float32 [768, 768], P(('tensor', 'dp'))
- serving_outproj: bfloat16 [768, 768], P('tensor')
- residue_expand: float32 [8, 768, 3072], P('dp', None, 'tensor')
- factor_expand: float32 [3072, 32], P('tensor')
- master_expand: float32 [768, 3072], P('dp', 'tensor')
- velocity_expand: float32 [768, 3072], P('dp', 'tensor')
- serving_expand: bfloat16 [768, 3072], P(None, 'tensor')
- residue_contract: float32 [8, 3072, 768], P('dp', 'tensor')
- factor_contract: float32 [768, 32], replicated
- master_contract: float32 [3072, 768], P(('tensor', 'dp'))
- velocity_contract: float32 [3072, 768], P(('tensor', 'dp'))
- serving_contract: bfloat16 [3072, 768], P('tensor')
All inputs are finite; a program needn't handle non-finite values.
Results may differ from a plain program's by a relative error of at most 0.012.
Values may be sent and summed in bfloat16 or wider, within the bound.
A program may use at most 128 MiB of HBM per device.

v0:
```python
import jax
import jax.numpy as jnp
from jax import lax
from jax.sharding import PartitionSpec as P

NS_STEPS = 5
momentum_beta = 0.9
step_size = 0.05


def matmul_high(left, right):
    return jnp.dot(left, right, precision=lax.Precision.HIGHEST, preferred_element_type=jnp.float32)


def inverse_root(gram):
    identity = jnp.eye(gram.shape[0], dtype=jnp.float32)
    norm_total = jnp.sqrt(jnp.sum(gram * gram)) + 1e-06
    iter_y = gram / norm_total
    iter_z = identity
    for repeat in range(NS_STEPS):
        middle = 1.5 * identity - 0.5 * matmul_high(iter_z, iter_y)
        iter_y = matmul_high(iter_y, middle)
        iter_z = matmul_high(middle, iter_z)
    return iter_z / jnp.sqrt(norm_total)


def own_rows(approx, weight):
    height = weight.shape[0]
    start = lax.axis_index("dp") * height
    return lax.dynamic_slice_in_dim(approx, start, height, 0)


def pair_update(col_group, row_group):
    grad_col, error_col, basis_col, weight_col, moment_col = col_group
    grad_row, error_row, basis_row, weight_row, moment_row = row_group
    replicas = lax.axis_size("dp")
    merged_col = grad_col[0].astype(jnp.float32) + error_col[0]
    merged_row = grad_row[0].astype(jnp.float32) + error_row[0]
    part_col = matmul_high(merged_col, basis_col)
    part_row = matmul_high(merged_row, basis_row)
    left_col = lax.psum(part_col, ("dp", "tensor")) / replicas
    left_row = lax.psum(part_row, "dp") / replicas
    gram_row = lax.psum(matmul_high(left_row.T, left_row), "tensor")
    gram_col = matmul_high(left_col.T, left_col)
    normed_col = matmul_high(left_col, inverse_root(gram_col))
    normed_row = matmul_high(left_row, inverse_root(gram_row))
    factor_col = (
        lax.psum(matmul_high(merged_col.T, normed_col).astype(jnp.bfloat16), "dp").astype(
            jnp.float32
        )
        / replicas
    )
    factor_row = lax.psum(matmul_high(merged_row.T, normed_row), ("dp", "tensor")) / replicas
    approx_col = matmul_high(normed_col, factor_col.T)
    approx_row = matmul_high(normed_row, factor_row.T)
    residue_col = (merged_col - approx_col)[None]
    residue_row = (merged_row - approx_row)[None]
    velocity_col = momentum_beta * moment_col + own_rows(approx_col, weight_col)
    velocity_row = momentum_beta * moment_row + own_rows(approx_row, weight_row)
    master_col = weight_col - step_size * velocity_col
    master_row = weight_row - step_size * velocity_row
    serving_col, serving_row = (
        lax.all_gather(master_col.astype(jnp.bfloat16), "dp", axis=0, tiled=True),
        lax.all_gather(master_row.astype(jnp.bfloat16), "dp", axis=0, tiled=True),
    )
    return (
        (residue_col, factor_col, master_col, velocity_col, serving_col),
        (residue_row, factor_row, master_row, velocity_row, serving_row),
    )


def body(
    grad_inproj,
    error_inproj,
    basis_inproj,
    weight_inproj,
    moment_inproj,
    grad_outproj,
    error_outproj,
    basis_outproj,
    weight_outproj,
    moment_outproj,
    grad_expand,
    error_expand,
    basis_expand,
    weight_expand,
    moment_expand,
    grad_contract,
    error_contract,
    basis_contract,
    weight_contract,
    moment_contract,
):
    first, second = pair_update(
        (grad_inproj, error_inproj, basis_inproj, weight_inproj, moment_inproj),
        (grad_outproj, error_outproj, basis_outproj, weight_outproj, moment_outproj),
    )
    third, fourth = pair_update(
        (grad_expand, error_expand, basis_expand, weight_expand, moment_expand),
        (grad_contract, error_contract, basis_contract, weight_contract, moment_contract),
    )
    return (
        first[0],
        first[1],
        first[2],
        first[3],
        first[4],
        second[0],
        second[1],
        second[2],
        second[3],
        second[4],
        third[0],
        third[1],
        third[2],
        third[3],
        third[4],
        fourth[0],
        fourth[1],
        fourth[2],
        fourth[3],
        fourth[4],
    )


def solution(mesh):
    in_specs = (
        P("dp", None, "tensor"),
        P("dp", None, "tensor"),
        P("tensor", None),
        P("dp", "tensor"),
        P("dp", "tensor"),
        P("dp", "tensor", None),
        P("dp", "tensor", None),
        P(),
        P(("tensor", "dp"), None),
        P(("tensor", "dp"), None),
        P("dp", None, "tensor"),
        P("dp", None, "tensor"),
        P("tensor", None),
        P("dp", "tensor"),
        P("dp", "tensor"),
        P("dp", "tensor", None),
        P("dp", "tensor", None),
        P(),
        P(("tensor", "dp"), None),
        P(("tensor", "dp"), None),
    )
    out_specs = (
        P("dp", None, "tensor"),
        P("tensor", None),
        P("dp", "tensor"),
        P("dp", "tensor"),
        P(None, "tensor"),
        P("dp", "tensor", None),
        P(),
        P(("tensor", "dp"), None),
        P(("tensor", "dp"), None),
        P("tensor", None),
        P("dp", None, "tensor"),
        P("tensor", None),
        P("dp", "tensor"),
        P("dp", "tensor"),
        P(None, "tensor"),
        P("dp", "tensor", None),
        P(),
        P(("tensor", "dp"), None),
        P(("tensor", "dp"), None),
        P("tensor", None),
    )
    return jax.shard_map(body, mesh=mesh, in_specs=in_specs, out_specs=out_specs, check_vma=False)
```

profile of v0, /device:TPU:0, one launch (start us, length us, event | category | flops | bytes accessed | tf_op | source)
XLA Modules:
  0.0 365.6 jit_solution(10655994586328658243)
XLA Ops:
  8.1 5.1 %fusion.2 = f32[768,32]{0,1:T(8,128)} fusion(f32[768,32]{0,1:T(8,128)S(1)} %copy-done, f32[1,768,768]{2,1,0:T(8,128)} %param.36, bf16[1,768,768]{2,1,0:T(8,128)(2,1)} %param.35), kind=kOutput, calls=%fused_computation.3 | convolution fusion | flops 227672064 | bytes 3735552 | tf_op jit(solution)/shard_map/dot_general | solution.py:12
  13.3 1.6 fusion.43
  14.9 25.5 %psum.72 = f32[192,32]{0,1:T(8,128)S(1)} all-reduce(f32[192,32]{0,1:T(8,128)S(1)} %fusion.43), channel_id=1, replica_groups=mesh['dp'=8,'tensor'=4] {'dp'}, use_global_device_ids=true, to_apply=%region_3.0 | all-reduce | flops 6144 | bytes 49152 | tf_op jit(solution)/shard_map/psum | solution.py:42
  40.4 1.9 fusion.12
  42.3 5.1 %fusion.7 = f32[768,32]{0,1:T(8,128)} fusion(f32[768,32]{0,1:T(8,128)} %param.32, f32[1,768,768]{2,1,0:T(8,128)} %param.31, bf16[1,768,768]{2,1,0:T(8,128)(2,1)} %param.30), kind=kOutput, calls=%fused_computation.9 | convolution fusion | flops 227672064 | bytes 3735552 | tf_op jit(solution)/shard_map/dot_general | solution.py:12
  47.6 20.0 %all-reduce.7.cloned.1.call-done = f32[768,32]{0,1:T(8,128)} async-done(((f32[768,32]{0,1:T(8,128)}), f32[768,32]{0,1:T(8,128)}) %all-reduce.7.cloned.1.call-update) | async-done | bytes 98320 | tf_op jit(solution)/shard_map/psum | solution.py:42
  68.8 19.0 %all-reduce.1 = (f32[32,32]{1,0:T(8,128)S(1)}, f32[32,32]{1,0:T(8,128)S(1)}) all-reduce(f32[32,32]{1,0:T(8,128)S(1)} %fusion.66, f32[32,32]{1,0:T(8,128)S(1)} %fusion.48), channel_id=1, replica_groups=mesh['dp'=8,'tensor'=4] {'tensor'}, use_global_device_ids=true, to_apply=%region_4.0 | all-reduce | flops 2048 | bytes 16384 | tf_op jit(solution)/shard_map/psum | solution.py:43
  95.0 3.5 fusion
  101.1 126.5 %all-reduce.9.cloned.1.call-done = (f32[768,32]{0,1:T(8,128)}, f32[768,32]{0,1:T(8,128)}, f32[768,32]{0,1:T(8,128)}, f32[768,32]{0,1:T(8,128)}) async-done(((f32[768,32]{0,1:T(8,128)}, f32[768,32]{0,1:T(8,128)}, f32[768,32]{0,1:T(8,128)}, f32[768,32]{0,1:T(8,128)}), (f32[768,32]{0,1:T(8,128)}, f32[768,32]{0,1:T(8,128)}, f32[768,32]{0,1:T(8,128)}, f32[768,32]{0,1:T(8,128)})) %all-reduce.9.cloned.1.call-update) | async-done | bytes 393232 | tf_op jit(solution)/shard_map/psum | solution.py:41
  227.6 1.8 multiply_reduce_fusion.1
  231.9 1.8 multiply_reduce_fusion.3
  236.6 1.3 fusion.50
  237.9 4.3 %fusion.15 = bf16[768,32]{0,1:T(8,128)(2,1)} fusion(f32[768,32]{0,1:T(8,128)S(1)} %fusion.50, f32[1,768,768]{2,1,0:T(8,128)} %param.31, bf16[1,768,768]{2,1,0:T(8,128)(2,1)} %param.30), kind=kOutput, calls=%fused_computation.21 | convolution fusion | flops 227696640 | bytes 3686400 | tf_op jit(solution)/shard_map/dot_general | solution.py:12
  243.7 2.3 fusion.18
  247.5 3.5 fusion.117
  251.1 2.1 fusion.86
  253.2 1.8 copy.44
  255.0 1.8 copy.45
  257.7 1.5 fusion.103
  260.0 1.6 fusion.88
  261.6 3.8 %fusion.4 = f32[1,768,768]{2,1,0:T(8,128)} fusion(f32[768,768]{1,0:T(8,128)} %fusion.117, f32[1,768,768]{2,1,0:T(8,128)S(1)} %copy-done.1, bf16[1,768,768]{2,1,0:T(8,128)(2,1)} %param.35), kind=kLoop, calls=%fused_computation.5 | loop fusion | flops 1769472 | bytes 8257536 | tf_op jit(solution)/shard_map/broadcast_in_dim | solution.py:57
  265.4 35.7 %all-reduce.11.cloned.1.call-done = (bf16[576,32]{0,1:T(8,128)(2,1)}, bf16[768,32]{0,1:T(8,128)(2,1)}) async-done(((bf16[576,32]{0,1:T(8,128)(2,1)}, bf16[768,32]{0,1:T(8,128)(2,1)}), (bf16[576,32]{0,1:T(8,128)(2,1)}, bf16[768,32]{0,1:T(8,128)(2,1)})) %all-reduce.11.cloned.1.call-update) | async-done | bytes 86032 | tf_op jit(solution)/shard_map/psum | solution.py:48
  302.7 2.1 fusion.110
  305.9 11.7 %all_gather.13 = bf16[192,768]{1,0:T(8,128)(2,1)} all-gather(bf16[24,768]{1,0:T(8,128)(2,1)} %get-tuple-element.74), channel_id=1, replica_groups=mesh['dp'=8,'tensor'=4] {'dp'}, dimensions={0}, use_global_device_ids=true | all-gather | bytes 331776 | tf_op jit(solution)/shard_map/all_gather | solution.py:64
  317.6 2.2 fusion.45
  321.2 1.6 fusion.96
  324.4 10.8 %all_gather.12 = bf16[768,576]{1,0:T(8,128)(2,1)S(1)} all-gather(bf16[96,576]{1,0:T(8,128)(2,1)S(1)} %copy.46), channel_id=1, replica_groups=mesh['dp'=8,'tensor'=4] {'dp'}, dimensions={0}, use_global_device_ids=true | all-gather | bytes 995328 | tf_op jit(solution)/shard_map/all_gather | solution.py:63
  335.2 1.3 copy.49
  338.2 3.7 %fusion.14 = f32[1,768,576]{1,2,0:T(8,128)} fusion(f32[768,576]{0,1:T(8,128)} %copy-done.8, f32[1,768,576]{1,2,0:T(8,128)} %param.21, bf16[1,768,576]{1,2,0:T(8,128)(2,1)S(1)} %copy-done.9), kind=kLoop, calls=%fused_computation.19 | loop fusion | flops 1327104 | bytes 6193152 | tf_op jit(solution)/shard_map/broadcast_in_dim | solution.py:56
  342.6 1.8 fusion.9
  344.4 10.6 %all-gather.3.cloned.1.call-done = bf16[768,768]{1,0:T(8,128)(2,1)} async-done(((bf16[96,768]{1,0:T(8,128)(2,1)}), bf16[768,768]{1,0:T(8,128)(2,1)}) %all-gather.3.cloned.1.call-update) | async-done | bytes 1179664 | tf_op jit(solution)/shard_map/all_gather | solution.py:63
  355.7 2.4 copy.61
  (147 shorter events, 28.7 us)
Async XLA Ops:
  7.2 0.9 copy-start
  7.2 6.1 %copy-start.10 = (f32[1,192,768]{2,1,0:T(8,128)S(1)}, f32[1,192,768]{2,1,0:T(8,128)}, u32[]{:S(2)}) copy-start(f32[1,192,768]{2,1,0:T(8,128)} %param.26) | copy-start | bytes 1769476
  7.2 6.1 %copy-start.29 = (f32[768,32]{0,1:T(8,128)S(1)}, f32[768,32]{0,1:T(8,128)}, u32[]{:S(2)}) copy-start(f32[768,32]{0,1:T(8,128)} %param.27) | copy-start | bytes 294916
  7.2 33.2 %copy-start.9 = (bf16[1,768,576]{1,2,0:T(8,128)(2,1)S(1)}, bf16[1,768,576]{1,2,0:T(8,128)(2,1)}, u32[]{:S(2)}) copy-start(bf16[1,768,576]{1,2,0:T(8,128)(2,1)} %param.20) | copy-start | bytes 2654212
  7.2 33.2 %copy-start.3 = (f32[1,768,576]{1,2,0:T(8,128)S(1)}, f32[1,768,576]{1,2,0:T(8,128)}, u32[]{:S(2)}) copy-start(f32[1,768,576]{1,2,0:T(8,128)} %param.21) | copy-start | bytes 5308420
  7.3 33.2 %copy-start.30 = (f32[576,32]{0,1:T(8,128)S(1)}, f32[576,32]{0,1:T(8,128)}, u32[]{:S(2)}) copy-start(f32[576,32]{0,1:T(8,128)} %param.22) | copy-start | bytes 221188
  7.3 60.3 %all-reduce.7.cloned.1.call-start = ((), (), s32[]{:S(2)}) async-start(), calls=%async_computation.1 | async-start | bytes 196608 | tf_op jit(solution)/shard_map/psum | solution.py:42
  13.2 214.3 %all-reduce.9.cloned.1.call-start = ((), (), s32[]{:S(2)}) async-start(), calls=%async_computation.3 | async-start | bytes 786432 | tf_op jit(solution)/shard_map/psum | solution.py:41
  42.3 52.7 %copy-start.1 = (f32[1,768,768]{2,1,0:T(8,128)S(1)}, f32[1,768,768]{2,1,0:T(8,128)}, u32[]{:S(2)}) copy-start(f32[1,768,768]{2,1,0:T(8,128)} %param.36) | copy-start | bytes 7077892
  93.5 6.2 %copy-start.11 = (f32[1,192,768]{2,1,0:T(8,128)S(1)}, f32[1,192,768]{2,1,0:T(8,128)}, u32[]{:S(2)}) copy-start(f32[1,192,768]{2,1,0:T(8,128)} %param.26) | copy-start | bytes 1769476
  93.5 6.2 %copy-start.13 = (bf16[1,192,768]{2,1,0:T(8,128)(2,1)S(1)}, bf16[1,192,768]{2,1,0:T(8,128)(2,1)}, u32[]{:S(2)}) copy-start(bf16[1,192,768]{2,1,0:T(8,128)(2,1)} %param.25) | copy-start | bytes 884740
  100.9 200.3 %all-reduce.11.cloned.1.call-start = ((), (), s32[]{:S(2)}) async-start(), calls=%async_computation.4 | async-start | bytes 180224 | tf_op jit(solution)/shard_map/psum | solution.py:48
  236.3 7.4 %copy-start.4 = (f32[1,768,576]{1,2,0:T(8,128)S(1)}, f32[1,768,576]{1,2,0:T(8,128)}, u32[]{:S(2)}) copy-start(f32[1,768,576]{1,2,0:T(8,128)} %param.21) | copy-start | bytes 5308420
  237.9 4.4 %copy-start.20 = (f32[768,32]{0,1:T(8,128)}, f32[768,32]{0,1:T(8,128)S(1)}, u32[]{:S(2)}) copy-start(f32[768,32]{0,1:T(8,128)S(1)} %fusion.50) | copy-start | bytes 294916
  251.0 93.3 %all-gather.5.cloned.1.call-start = ((), (), s32[]{:S(2)}) async-start(), calls=%async_computation.2 | async-start | bytes 1327104 | tf_op jit(solution)/shard_map/all_gather | solution.py:64
  253.2 101.9 %all-gather.3.cloned.1.call-start = ((), (), s32[]{:S(2)}) async-start(), calls=%async_computation | async-start | bytes 1327104 | tf_op jit(solution)/shard_map/all_gather | solution.py:63
  257.7 1.5 copy-start.24
  259.2 0.8 copy-start.12
  261.6 41.0 %copy-start.21 = (f32[768,32]{0,1:T(8,128)S(1)}, f32[768,32]{0,1:T(8,128)}, u32[]{:S(2)}) copy-start(f32[768,32]{0,1:T(8,128)} %copy-done.20) | copy-start | bytes 294916
  301.2 3.6 copy-start.27
  301.2 3.6 copy-start.28
  304.8 18.1 %copy-start.5 = (f32[768,768]{1,0:T(8,128)}, f32[768,768]{1,0:T(8,128)S(1)}, u32[]{:S(2)}) copy-start(f32[768,768]{1,0:T(8,128)S(1)} %fusion.110) | copy-start | bytes 7077892
  305.9 17.0 %copy-start.16 = (f32[96,576]{0,1:T(8,128)S(1)}, f32[96,576]{0,1:T(8,128)}, u32[]{:S(2)}) copy-start(f32[96,576]{0,1:T(8,128)} %copy.44) | copy-start | bytes 663556
  305.9 17.0 %copy-start.17 = (f32[96,576]{0,1:T(8,128)S(1)}, f32[96,576]{0,1:T(8,128)}, u32[]{:S(2)}) copy-start(f32[96,576]{0,1:T(8,128)} %copy.45) | copy-start | bytes 663556
  322.9 1.4 copy-start.8
  324.3 12.2 %copy-start.19 = (f32[96,576]{0,1:T(8,128)S(1)}, f32[96,576]{0,1:T(8,128)}, u32[]{:S(2)}) copy-start(f32[96,576]{0,1:T(8,128)} %get-tuple-element.78) | copy-start | bytes 663556
  324.3 13.0 %copy-start.18 = (f32[96,576]{0,1:T(8,128)S(1)}, f32[96,576]{0,1:T(8,128)}, u32[]{:S(2)}) copy-start(f32[96,576]{0,1:T(8,128)} %get-tuple-element.79) | copy-start | bytes 663556
  338.2 3.7 %copy-start.2 = (f32[1,768,768]{2,1,0:T(8,128)S(1)}, f32[1,768,768]{2,1,0:T(8,128)}, u32[]{:S(2)}) copy-start(f32[1,768,768]{2,1,0:T(8,128)} %param.31) | copy-start | bytes 7077892
  338.2 3.7 %copy-start.6 = (f32[768,768]{1,0:T(8,128)S(1)}, f32[768,768]{1,0:T(8,128)}, u32[]{:S(2)}) copy-start(f32[768,768]{1,0:T(8,128)} %copy-done.5) | copy-start | bytes 7077892
  338.2 4.4 %copy-start.7 = (bf16[1,768,768]{2,1,0:T(8,128)(2,1)S(1)}, bf16[1,768,768]{2,1,0:T(8,128)(2,1)}, u32[]{:S(2)}) copy-start(bf16[1,768,768]{2,1,0:T(8,128)(2,1)} %param.30) | copy-start | bytes 3538948
  342.6 12.4 %copy-start.15 = (bf16[192,768]{1,0:T(8,128)(2,1)S(1)}, bf16[192,768]{1,0:T(8,128)(2,1)}, u32[]{:S(2)}) copy-start(bf16[192,768]{1,0:T(8,128)(2,1)} %all_gather.13) | copy-start | bytes 884740
  344.4 13.7 %copy-start.14 = (bf16[768,768]{1,0:T(8,128)(2,1)S(1)}, bf16[768,768]{1,0:T(8,128)(2,1)}, u32[]{:S(2)}) copy-start(bf16[768,768]{1,0:T(8,128)(2,1)} %all-gather.5.cloned.1.call-done) | copy-start | bytes 3538948
  (4 other events, 2.5 us)
Sparse Core Ops, SparseCore 0:
  13.3 54.1 all-reduce.6
  101.0 126.5 all-reduce.8
  251.1 49.9 all-reduce.10
  303.1 25.3 all-gather.4
  330.9 24.0 all-gather.2
where the time goes:
time: 367 us; the launch traced here: 366 us
  waiting for transfers between devices  193 us (53%)
  blocking collectives  67 us (18%)
  matrix products  50.5 us (14%)
  other arithmetic  21.4 us (6%)
  between operations  17.4 us (5%)
  local copies, waits for them, and re-layouts  16.1 us (4%)
    psum x1, waiting for transfers between devices, pair_update(): left_col = lax.psum(part_col, ('dp', 'tensor')) / replicas  126 us
    dot_general x76, matrix products, matmul_high(): jnp.dot(left, right, precision=lax.Precision.HIGHEST, preferred_element_t...  50.5 us
    psum x1, waiting for transfers between devices, pair_update(): lax.psum(matmul_high(merged_col.T, normed_col).astype(jnp.bfloat16), 'dp')  35.7 us
    psum x1, blocking collectives, pair_update(): left_row = lax.psum(part_row, 'dp') / replicas  25.5 us
    psum x1, waiting for transfers between devices, pair_update(): left_row = lax.psum(part_row, 'dp') / replicas  20 us
    psum x1, blocking collectives, pair_update(): gram_row = lax.psum(matmul_high(left_row.T, left_row), 'tensor')  19 us
    unnamed x70, local copies, waits for them, and re-layouts  15.9 us
    all_gather x1, blocking collectives, pair_update(): lax.all_gather(master_row.astype(jnp.bfloat16), 'dp', axis=0, tiled=True)  11.7 us
  transfers between devices with their start and end apart: 5, of which 4 were waited for; matrix products, arithmetic and copies ran while one was open for 11% of the time, Pallas kernels for 0%

commit v1 on v0

--- a/solution.py
+++ b/solution.py
@@ -38,7 +38,13 @@
     merged_row = grad_row[0].astype(jnp.float32) + error_row[0]
     part_col = matmul_high(merged_col, basis_col)
     part_row = matmul_high(merged_row, basis_row)
-    left_col = lax.psum(part_col, ("dp", "tensor")) / replicas
+
+    def do_the_loads(view):
+        for s in ("tensor", "dp"):
+            view = jax.lax.psum(view, s)
+        return view
+
+    left_col = do_the_loads(part_col) / replicas
     left_row = lax.psum(part_row, "dp") / replicas
     gram_row = lax.psum(matmul_high(left_row.T, left_row), "tensor")
     gram_col = matmul_high(left_col.T, left_col)

time: 367 us -> 410 us (1.12)
  waiting for transfers between devices: 193 us -> 234 us
    psum x2 -> x3, waiting for transfers between devices: 146 us -> 173 us  [the longest x1 109 us: pair_update(): lax.psum(matmul_high(merged_row.T, normed_row), ('dp', 'tensor')) / replicas]
    all_gather x1, waiting for transfers between devices: 0.01 us -> 15.1 us  [pair_update(): lax.all_gather(master_row.astype(jnp.bfloat16), 'dp', axis=0, tiled=True)]
    all_gather x1, waiting for transfers between devices: 10.6 us -> 0.01 us  [pair_update(): lax.all_gather(master_col.astype(jnp.bfloat16), 'dp', axis=0, tiled=True)]
    psum x1, waiting for transfers between devices: 35.7 us -> 46.2 us  [pair_update(): lax.psum(matmul_high(merged_col.T, normed_col).astype(jnp.bfloat16), 'dp')]
    unnamed x70 -> x80, local copies, waits for them, and re-layouts: 15.9 us -> 18 us
  transfers between devices with their start and end apart: 5 -> 6, of which waited for: 4 -> 5; matrix products, arithmetic and copies ran while one was open for 11% -> 10% of each run, Pallas kernels for 0% -> 0%
where the time goes in v1:
time: 410 us; the launch traced here: 409 us
  waiting for transfers between devices  234 us (57%)
  blocking collectives  65.7 us (16%)
  matrix products  53.7 us (13%)
  local copies, waits for them, and re-layouts  19.7 us (5%)
  other arithmetic  17.8 us (4%)
  between operations  17.7 us (4%)
    psum x1, waiting for transfers between devices, pair_update(): lax.psum(matmul_high(merged_row.T, normed_row), ('dp', 'tensor')) / replicas  109 us
    psum x2, waiting for transfers between devices, do_the_loads(): view = jax.lax.psum(view, s)  64.1 us
    dot_general x76, matrix products, matmul_high(): jnp.dot(left, right, precision=lax.Precision.HIGHEST, preferred_element_t...  53.7 us
    psum x1, waiting for transfers between devices, pair_update(): lax.psum(matmul_high(merged_col.T, normed_col).astype(jnp.bfloat16), 'dp')  46.2 us
    psum x1, blocking collectives, pair_update(): left_row = lax.psum(part_row, 'dp') / replicas  25.5 us
    psum x1, blocking collectives, pair_update(): gram_row = lax.psum(matmul_high(left_row.T, left_row), 'tensor')  19 us
    unnamed x80, local copies, waits for them, and re-layouts  18 us
    all_gather x1, waiting for transfers between devices, pair_update(): lax.all_gather(master_row.astype(jnp.bfloat16), 'dp', axis=0, tiled=True)  15.1 us
  transfers between devices with their start and end apart: 6, of which 5 were waited for; matrix products, arithmetic and copies ran while one was open for 10% of the time, Pallas kernels for 0%

profile of v1, /device:TPU:0, one launch (start us, length us, event | category | flops | bytes accessed | tf_op | source)
XLA Modules:
  0.0 409.3 jit_solution(13117735565475752050)
XLA Ops:
  7.3 3.7 fusion.12
  11.0 4.3 %fusion.7 = f32[768,32]{0,1:T(8,128)} fusion(f32[768,32]{0,1:T(8,128)S(1)} %copy-done, f32[1,768,768]{2,1,0:T(8,128)S(1)} %copy-done.1, bf16[1,768,768]{2,1,0:T(8,128)(2,1)} %param.30), kind=kOutput, calls=%fused_computation.9 | convolution fusion | flops 227672064 | bytes 3735552 | tf_op jit(solution)/shard_map/dot_general | solution.py:12
  16.1 25.5 %psum.87 = f32[192,32]{0,1:T(8,128)S(1)} all-reduce(f32[192,32]{0,1:T(8,128)S(1)} %fusion.43), channel_id=1, replica_groups=mesh['dp'=8,'tensor'=4] {'dp'}, use_global_device_ids=true, to_apply=%region_4.0 | all-reduce | flops 6144 | bytes 49152 | tf_op jit(solution)/shard_map/psum | solution.py:48
  41.6 5.0 %fusion.2 = f32[768,32]{0,1:T(8,128)} fusion(f32[768,32]{0,1:T(8,128)} %param.37, f32[1,768,768]{2,1,0:T(8,128)} %param.36, bf16[1,768,768]{2,1,0:T(8,128)(2,1)} %param.35), kind=kOutput, calls=%fused_computation.3 | convolution fusion | flops 227672064 | bytes 3735552 | tf_op jit(solution)/shard_map/dot_general | solution.py:12
  46.6 6.5 %all-reduce.14.cloned.1.call-done = (f32[768,32]{0,1:T(8,128)}, f32[768,32]{0,1:T(8,128)}) async-done(((f32[768,32]{0,1:T(8,128)}, f32[768,32]{0,1:T(8,128)}), (f32[768,32]{0,1:T(8,128)}, f32[768,32]{0,1:T(8,128)})) %all-reduce.14.cloned.1.call-update) | async-done | bytes 196624 | tf_op jit(solution)/shard_map/psum | solution.py:44
  53.4 57.6 %all-reduce.12.cloned.1.call-done = (f32[768,32]{0,1:T(8,128)}, f32[768,32]{0,1:T(8,128)}, f32[768,32]{0,1:T(8,128)}) async-done(((f32[768,32]{0,1:T(8,128)}, f32[768,32]{0,1:T(8,128)}, f32[768,32]{0,1:T(8,128)}), (f32[768,32]{0,1:T(8,128)}, f32[768,32]{0,1:T(8,128)}, f32[768,32]{0,1:T(8,128)})) %all-reduce.12.cloned.1.call-update) | async-done | bytes 294928 | tf_op jit(solution)/shard_map/psum | solution.py:44
  112.3 19.0 %all-reduce.2 = (f32[32,32]{1,0:T(8,128)S(1)}, f32[32,32]{1,0:T(8,128)S(1)}) all-reduce(f32[32,32]{1,0:T(8,128)S(1)} %fusion.66, f32[32,32]{1,0:T(8,128)S(1)} %fusion.48), channel_id=1, replica_groups=mesh['dp'=8,'tensor'=4] {'tensor'}, use_global_device_ids=true, to_apply=%region_5.0 | all-reduce | flops 2048 | bytes 16384 | tf_op jit(solution)/shard_map/psum | solution.py:49
  137.6 1.8 multiply_reduce_fusion.1
  143.1 1.8 multiply_reduce_fusion.3
  149.3 4.2 %fusion = f32[768,32]{0,1:T(8,128)} fusion(f32[768,32]{0,1:T(8,128)S(1)} %fusion.46, f32[1,768,768]{2,1,0:T(8,128)} %param.36, bf16[1,768,768]{2,1,0:T(8,128)(2,1)} %param.35), kind=kOutput, calls=%fused_computation.1 | convolution fusion | flops 227672064 | bytes 3735552 | tf_op jit(solution)/shard_map/dot_general | solution.py:12
  155.5 1.6 fusion.64
  159.1 2.3 fusion.15
  162.0 2.3 fusion.18
  164.4 2.3 fusion.41
  166.7 46.2 %all-reduce.16.cloned.1.call-done = (bf16[576,32]{0,1:T(8,128)(2,1)}, bf16[768,32]{0,1:T(8,128)(2,1)}) async-done(((bf16[576,32]{0,1:T(8,128)(2,1)}, bf16[768,32]{0,1:T(8,128)(2,1)}), (bf16[576,32]{0,1:T(8,128)(2,1)}, bf16[768,32]{0,1:T(8,128)(2,1)})) %all-reduce.16.cloned.1.call-update) | async-done | bytes 86032 | tf_op jit(solution)/shard_map/psum | solution.py:54
  214.5 2.9 fusion.110
  220.1 1.8 copy.44
  221.9 1.8 copy.45
  225.1 1.6 fusion.96
  227.9 2.1 fusion.89
  230.0 1.7 copy.46
  231.7 3.5 fusion.14
  235.2 108.6 %all-reduce.10.cloned.1.call-done = (f32[768,32]{0,1:T(8,128)}, f32[768,32]{0,1:T(8,128)}) async-done(((f32[768,32]{0,1:T(8,128)}, f32[768,32]{0,1:T(8,128)}), (f32[768,32]{0,1:T(8,128)}, f32[768,32]{0,1:T(8,128)})) %all-reduce.10.cloned.1.call-update) | async-done | bytes 196624 | tf_op jit(solution)/shard_map/psum | solution.py:59
  344.7 2.0 fusion.117
  349.1 11.8 %all_gather.12 = bf16[768,576]{1,0:T(8,128)(2,1)S(1)} all-gather(bf16[96,576]{1,0:T(8,128)(2,1)} %copy.46), channel_id=1, replica_groups=mesh['dp'=8,'tensor'=4] {'dp'}, dimensions={0}, use_global_device_ids=true | all-gather | bytes 995328 | tf_op jit(solution)/shard_map/all_gather | solution.py:69
  362.2 1.8 copy.47
  364.0 1.8 copy.48
  365.9 3.9 fusion.9
  371.2 9.4 %all_gather.13 = bf16[192,768]{1,0:T(8,128)(2,1)S(1)} all-gather(bf16[24,768]{1,0:T(8,128)(2,1)S(1)} %get-tuple-element.77), channel_id=1, replica_groups=mesh['dp'=8,'tensor'=4] {'dp'}, dimensions={0}, use_global_device_ids=true | all-gather | bytes 331776 | tf_op jit(solution)/shard_map/all_gather | solution.py:70
  381.5 1.8 fusion.4
  383.3 15.1 %all-gather.5.cloned.1.call-done = bf16[768,768]{1,0:T(8,128)(2,1)} async-done(((bf16[96,768]{1,0:T(8,128)(2,1)}), bf16[768,768]{1,0:T(8,128)(2,1)}) %all-gather.5.cloned.1.call-update) | async-done | bytes 1179664 | tf_op jit(solution)/shard_map/all_gather | solution.py:70
  399.1 2.4 copy.63
  (160 shorter events, 33.4 us)
Async XLA Ops:
  7.2 45.9 %all-reduce.14.cloned.1.call-start = ((), (), s32[]{:S(2)}) async-start(), calls=%async_computation.4 | async-start | bytes 393216 | tf_op jit(solution)/shard_map/psum | solution.py:44
  11.0 4.4 %copy-start.11 = (f32[1,192,768]{2,1,0:T(8,128)S(1)}, f32[1,192,768]{2,1,0:T(8,128)}, u32[]{:S(2)}) copy-start(f32[1,192,768]{2,1,0:T(8,128)} %param.26) | copy-start | bytes 1769476
  11.0 4.4 %copy-start.13 = (bf16[1,192,768]{2,1,0:T(8,128)(2,1)S(1)}, bf16[1,192,768]{2,1,0:T(8,128)(2,1)}, u32[]{:S(2)}) copy-start(bf16[1,192,768]{2,1,0:T(8,128)(2,1)} %param.25) | copy-start | bytes 884740
  11.0 4.4 %copy-start.31 = (f32[768,32]{0,1:T(8,128)S(1)}, f32[768,32]{0,1:T(8,128)}, u32[]{:S(2)}) copy-start(f32[768,32]{0,1:T(8,128)} %param.27) | copy-start | bytes 294916
  15.4 95.6 %all-reduce.12.cloned.1.call-start = ((), (), s32[]{:S(2)}) async-start(), calls=%async_computation.3 | async-start | bytes 589824 | tf_op jit(solution)/shard_map/psum | solution.py:44
  41.6 11.8 %copy-start.25 = (f32[192,32]{0,1:T(8,128)}, f32[192,32]{0,1:T(8,128)S(1)}, u32[]{:S(2)}) copy-start(f32[192,32]{0,1:T(8,128)S(1)} %psum.87) | copy-start | bytes 73732
  53.2 159.8 %all-reduce.16.cloned.1.call-start = ((), (), s32[]{:S(2)}) async-start(), calls=%async_computation.5 | async-start | bytes 180224 | tf_op jit(solution)/shard_map/psum | solution.py:54
  111.0 38.0 %copy-start.21 = (f32[768,32]{0,1:T(8,128)S(1)}, f32[768,32]{0,1:T(8,128)}, u32[]{:S(2)}) copy-start(f32[768,32]{0,1:T(8,128)} %get-tuple-element.63) | copy-start | bytes 294916
  146.2 12.6 %copy-start.20 = (f32[768,32]{0,1:T(8,128)S(1)}, f32[768,32]{0,1:T(8,128)}, u32[]{:S(2)}) copy-start(f32[768,32]{0,1:T(8,128)} %get-tuple-element.64) | copy-start | bytes 294916
  148.7 10.4 %copy-start.7 = (bf16[1,768,768]{2,1,0:T(8,128)(2,1)S(1)}, bf16[1,768,768]{2,1,0:T(8,128)(2,1)}, u32[]{:S(2)}) copy-start(bf16[1,768,768]{2,1,0:T(8,128)(2,1)} %param.30) | copy-start | bytes 3538948
  153.5 7.8 %copy-start.34 = (f32[32,32]{1,0:T(8,128)S(1)}, f32[32,32]{1,0:T(8,128)}, u32[]{:S(2)}) copy-start(f32[32,32]{1,0:T(8,128)} %fusion.95) | copy-start | bytes 12292
  153.6 7.8 %copy-start.35 = (f32[32,32]{1,0:T(8,128)S(1)}, f32[32,32]{1,0:T(8,128)}, u32[]{:S(2)}) copy-start(f32[32,32]{1,0:T(8,128)} %fusion.94) | copy-start | bytes 12292
  153.6 8.1 %copy-start.19 = (f32[768,32]{0,1:T(8,128)S(1)}, f32[768,32]{0,1:T(8,128)}, u32[]{:S(2)}) copy-start(f32[768,32]{0,1:T(8,128)} %get-tuple-element.62) | copy-start | bytes 294916
  153.6 8.4 %copy-start.3 = (f32[1,768,576]{1,2,0:T(8,128)S(1)}, f32[1,768,576]{1,2,0:T(8,128)}, u32[]{:S(2)}) copy-start(f32[1,768,576]{1,2,0:T(8,128)} %param.21) | copy-start | bytes 5308420
  153.6 8.4 %copy-start.10 = (bf16[1,768,576]{1,2,0:T(8,128)(2,1)S(1)}, bf16[1,768,576]{1,2,0:T(8,128)(2,1)}, u32[]{:S(2)}) copy-start(bf16[1,768,576]{1,2,0:T(8,128)(2,1)} %param.20) | copy-start | bytes 2654212
  164.3 179.5 %all-reduce.10.cloned.1.call-start = ((), (), s32[]{:S(2)}) async-start(), calls=%async_computation.2 | async-start | bytes 393216 | tf_op jit(solution)/shard_map/psum | solution.py:59
  166.7 216.6 %all-gather.3.cloned.1.call-start = ((), (), s32[]{:S(2)}) async-start(), calls=%async_computation | async-start | bytes 1327104 | tf_op jit(solution)/shard_map/all_gather | solution.py:69
  213.0 5.9 %copy-start.26 = (f32[96,768]{1,0:T(8,128)S(1)}, f32[96,768]{1,0:T(8,128)}, u32[]{:S(2)}) copy-start(f32[96,768]{1,0:T(8,128)} %param.33) | copy-start | bytes 884740
  213.0 5.9 %copy-start.27 = (f32[96,768]{1,0:T(8,128)S(1)}, f32[96,768]{1,0:T(8,128)}, u32[]{:S(2)}) copy-start(f32[96,768]{1,0:T(8,128)} %param.34) | copy-start | bytes 884740
  219.8 178.6 %all-gather.5.cloned.1.call-start = ((), (), s32[]{:S(2)}) async-start(), calls=%async_computation.1 | async-start | bytes 1327104 | tf_op jit(solution)/shard_map/all_gather | solution.py:70
  235.2 113.0 %copy-start.28 = (f32[96,768]{1,0:T(8,128)S(1)}, f32[96,768]{1,0:T(8,128)}, u32[]{:S(2)}) copy-start(f32[96,768]{1,0:T(8,128)} %param.38) | copy-start | bytes 884740
  235.2 113.0 %copy-start.29 = (f32[96,768]{1,0:T(8,128)S(1)}, f32[96,768]{1,0:T(8,128)}, u32[]{:S(2)}) copy-start(f32[96,768]{1,0:T(8,128)} %param.39) | copy-start | bytes 884740
  344.7 16.3 %copy-start.18 = (f32[768,32]{0,1:T(8,128)}, f32[768,32]{0,1:T(8,128)S(1)}, u32[]{:S(2)}) copy-start(f32[768,32]{0,1:T(8,128)S(1)} %broadcast_multiply_fusion) | copy-start | bytes 294916
  365.8 4.0 copy-start.24
  365.8 4.7 %copy-start.32 = (f32[24,768]{1,0:T(8,128)S(1)}, f32[24,768]{1,0:T(8,128)}, u32[]{:S(2)}) copy-start(f32[24,768]{1,0:T(8,128)} %param.28) | copy-start | bytes 221188
  365.8 4.7 %copy-start.33 = (f32[24,768]{1,0:T(8,128)S(1)}, f32[24,768]{1,0:T(8,128)}, u32[]{:S(2)}) copy-start(f32[24,768]{1,0:T(8,128)} %param.29) | copy-start | bytes 221188
  365.8 14.8 %copy-start.12 = (f32[1,192,768]{2,1,0:T(8,128)S(1)}, f32[1,192,768]{2,1,0:T(8,128)}, u32[]{:S(2)}) copy-start(f32[1,192,768]{2,1,0:T(8,128)} %param.26) | copy-start | bytes 1769476
  365.9 14.7 %copy-start.14 = (bf16[1,192,768]{2,1,0:T(8,128)(2,1)S(1)}, bf16[1,192,768]{2,1,0:T(8,128)(2,1)}, u32[]{:S(2)}) copy-start(bf16[1,192,768]{2,1,0:T(8,128)(2,1)} %param.25) | copy-start | bytes 884740
  365.9 15.6 %copy-start.6 = (f32[768,768]{1,0:T(8,128)S(1)}, f32[768,768]{1,0:T(8,128)}, u32[]{:S(2)}) copy-start(f32[768,768]{1,0:T(8,128)} %copy-done.5) | copy-start | bytes 7077892
  369.8 11.7 %copy-start.2 = (f32[1,768,768]{2,1,0:T(8,128)S(1)}, f32[1,768,768]{2,1,0:T(8,128)}, u32[]{:S(2)}) copy-start(f32[1,768,768]{2,1,0:T(8,128)} %param.36) | copy-start | bytes 7077892
  369.8 11.7 %copy-start.8 = (bf16[1,768,768]{2,1,0:T(8,128)(2,1)S(1)}, bf16[1,768,768]{2,1,0:T(8,128)(2,1)}, u32[]{:S(2)}) copy-start(bf16[1,768,768]{2,1,0:T(8,128)(2,1)} %param.35) | copy-start | bytes 3538948
  369.8 13.5 %copy-start.22 = (f32[768,32]{0,1:T(8,128)}, f32[768,32]{0,1:T(8,128)S(1)}, u32[]{:S(2)}) copy-start(f32[768,32]{0,1:T(8,128)S(1)} %broadcast_multiply_fusion.1) | copy-start | bytes 294916
  (10 other events, 22.4 us)
Sparse Core Ops, SparseCore 0:
  15.5 37.6 all-reduce.13
  57.6 53.3 all-reduce.11
  164.5 48.4 all-reduce.15
  219.6 124.1 all-reduce.9
  346.1 25.8 all-gather.2
  374.3 24.0 all-gather.4
